TPU v7x, 32 devices: a whole 2x2x4 slice. The times are simulated.
32 devices in a mesh: ctx: 16 (over z, x, core), head: 2 (over y).
Axes of the slice: x: 2, y: 2, z: 4, core: 2. Of those that a mesh axis runs over, the one named last changes fastest.
Arguments:
- latent: bfloat16 [6144, 5120], P('ctx', 'head'), may hold values from -6 to 6
- probe: bfloat16 [6144, 5120], P('ctx'), may hold values from -6 to 6
- norm_gain: float32 [5120], replicated, may hold values from 0.25 to 1.75
- w_query: bfloat16 [5120, 3072], P('ctx', 'head'), may hold values from -2 to 2, as said below
- w_key: bfloat16 [5120, 3072], P('ctx', 'head'), may hold values from -2 to 2, as said below
- w_value: bfloat16 [5120, 3072], P('ctx', 'head'), may hold values from -0.078125 to 0.078125
- w_out: bfloat16 [3072, 5120], P('head', 'ctx'), may hold values from -0.109375 to 0.109375
- tile_mask: int32 [48, 48], replicated, may hold values from 0 to 1, as said below
Outputs:
- mixed: bfloat16 [6144, 5120], P('ctx', 'head')
- branch_tangent: bfloat16 [6144, 5120], P('ctx', 'head')
- trace_terms: float32 [6144], P('ctx')
Inputs may be any that keep to these rules, and one draw needn't show every extreme that they name: `tile_mask`: entry [q, k] is 0 where |q - k| > 3, and 1 where q == k or |q - k| == 3. `w_query`: entries of order 5120^-0.5. `w_key`: entries of order 5120^-0.5.
All inputs are finite; a program needn't handle non-finite values.
Results may differ from a plain program's by a relative error of at most 0.011.
Values may be sent and summed in bfloat16 or wider, within the bound.
A program may use at most 192 MiB of HBM per device.

v0:
```python
import jax
import jax.numpy as jnp
from jax import lax
from jax.sharding import PartitionSpec as P

D = 5120
HD = 128
TILE = 128


def with_halo(block, sides, width):
    for axis, dim in sides:
        count = lax.axis_size(axis)
        forward = [(i, i + 1) for i in range(count - 1)]
        backward = [(target, source) for source, target in forward]
        low = lax.ppermute(
            lax.slice_in_dim(block, block.shape[dim] - width, None, axis=dim), axis, forward
        )
        high = lax.ppermute(lax.slice_in_dim(block, 0, width, axis=dim), axis, backward)
        block = jnp.concatenate([low, block, high], axis=dim)
    return block


def attend_block(queries, queries_t, keys, values, keys_t, values_t, allowed):
    score_scale = HD ** (-0.5)
    scores = (
        jnp.einsum("qhd,khd->hqk", queries, keys, preferred_element_type=jnp.float32) * score_scale
    )
    masked = jnp.where(allowed[None], scores, -jnp.inf)
    highest = jnp.max(masked, -1, keepdims=True)
    expos = jnp.exp(masked - highest)
    probs = expos / jnp.sum(expos, -1, keepdims=True)
    scores_t = jnp.einsum("qhd,khd->hqk", queries_t, keys, preferred_element_type=jnp.float32)
    scores_t = (
        scores_t + jnp.einsum("qhd,khd->hqk", queries, keys_t, preferred_element_type=jnp.float32)
    ) * score_scale
    probs_t = probs * (scores_t - jnp.sum(probs * scores_t, -1, keepdims=True))
    probs_b = probs.astype(jnp.bfloat16)
    probs_tb = probs_t.astype(jnp.bfloat16)
    attended = jnp.einsum(
        "hqk,khd->qhd", probs_b, values, preferred_element_type=jnp.float32
    ).astype(jnp.bfloat16)
    attended_t = jnp.einsum("hqk,khd->qhd", probs_b, values_t, preferred_element_type=jnp.float32)
    attended_t = (
        attended_t
        + jnp.einsum("hqk,khd->qhd", probs_tb, values, preferred_element_type=jnp.float32)
    ).astype(jnp.bfloat16)
    return (attended, attended_t)


def shards(latent, probe, norm_gain, w_query, w_key, w_value, w_out, tile_mask):
    tok_rows, own_cols = latent.shape
    head_cols = w_query.shape[1]
    col_start = lax.axis_index("head") * own_cols
    tangent_own = lax.dynamic_slice_in_dim(probe, col_start, own_cols, 1).astype(jnp.float32)
    latent_f = latent.astype(jnp.float32)
    gain_own = lax.dynamic_slice_in_dim(norm_gain, col_start, own_cols, 0)
    squares, crossed = lax.psum(
        (jnp.sum(latent_f * latent_f, -1), jnp.sum(latent_f * tangent_own, -1)), "head"
    )
    inverse = lax.rsqrt(squares[:, None] / D + 1e-06)
    along = crossed[:, None] / D
    normed_own = (latent_f * inverse * gain_own).astype(jnp.bfloat16)
    normed_t_own = ((tangent_own * inverse - latent_f * inverse**3 * along) * gain_own).astype(
        jnp.bfloat16
    )
    normed, normed_t = (
        lax.all_gather(normed_own, "head", axis=1, tiled=True),
        lax.all_gather(normed_t_own, "head", axis=1, tiled=True),
    )

    def add_rows(weight_rows):
        first = jnp.dot(normed, weight_rows, preferred_element_type=jnp.float32)
        second = jnp.dot(normed_t, weight_rows, preferred_element_type=jnp.float32)
        return (first, second)

    pair_query = add_rows(lax.all_gather(w_query, "ctx", axis=0, tiled=True))
    pair_key = add_rows(lax.all_gather(w_key, "ctx", axis=0, tiled=True))
    pair_value = add_rows(lax.all_gather(w_value, "ctx", axis=0, tiled=True))
    heads_dev = head_cols // HD
    query = pair_query[0].astype(jnp.bfloat16).reshape(tok_rows, heads_dev, HD)
    query_t = pair_query[1].astype(jnp.bfloat16).reshape(tok_rows, heads_dev, HD)
    stacked = jnp.stack(
        [
            pair_key[0].astype(jnp.bfloat16),
            pair_value[0].astype(jnp.bfloat16),
            pair_key[1].astype(jnp.bfloat16),
            pair_value[1].astype(jnp.bfloat16),
        ]
    )
    beside_all = with_halo(stacked, (("ctx", 1),), tok_rows)
    beside_all = beside_all.reshape(4, 3 * tok_rows, heads_dev, HD)
    tiles_dev = tok_rows // TILE
    ctx_slot = lax.axis_index("ctx")
    mask_pad = jnp.pad(tile_mask, tiles_dev)
    tile_rows = lax.dynamic_slice(
        mask_pad,
        (ctx_slot * tiles_dev + tiles_dev, ctx_slot * tiles_dev),
        (tiles_dev, 3 * tiles_dev),
    )
    allowed = jnp.repeat(jnp.repeat(tile_rows, TILE, 0), TILE, 1) == 1
    attended, attended_t = attend_block(
        query, query_t, beside_all[0], beside_all[1], beside_all[2], beside_all[3], allowed
    )
    both_rows = jnp.concatenate(
        [attended.reshape(tok_rows, head_cols), attended_t.reshape(tok_rows, head_cols)], 0
    )
    terms = jnp.dot(
        both_rows,
        lax.all_gather(w_out, "ctx", axis=1, tiled=True),
        preferred_element_type=jnp.float32,
    )
    summed = lax.psum_scatter(
        terms.astype(jnp.bfloat16), "head", scatter_dimension=1, tiled=True
    ).astype(jnp.float32)
    branch = summed[:tok_rows]
    branch_t = summed[tok_rows:]
    mixed = (latent_f + branch).astype(jnp.bfloat16)
    trace_terms = lax.psum(jnp.sum(tangent_own * branch_t, -1), "head")
    return (mixed, branch_t.astype(jnp.bfloat16), trace_terms)


def solution(mesh):
    placed = (
        P("ctx", "head"),
        P("ctx", None),
        P(),
        P("ctx", "head"),
        P("ctx", "head"),
        P("ctx", "head"),
        P("head", "ctx"),
        P(),
    )
    return jax.shard_map(
        shards,
        mesh=mesh,
        in_specs=placed,
        out_specs=(P("ctx", "head"), P("ctx", "head"), P("ctx")),
        check_vma=False,
    )
```

profile of v0, /device:TPU:0, one launch (start us, length us, event | category | flops | bytes accessed | tf_op | source)
XLA Modules:
  0.0 851.1 jit_solution(12549174765315246761)
XLA Ops:
  11.1 5.9 all-reduce.1
  26.1 52.3 %all-gather.7.cloned.1.call-done = bf16[384,5120]{1,0:T(8,128)(2,1)} async-done(((bf16[384,2560]{1,0:T(8,128)(2,1)}), bf16[384,5120]{1,0:T(8,128)(2,1)}) %all-gather.7.cloned.1.call-update) | async-done | bytes 3932176 | tf_op jit(solution)/shard_map/all_gather | solution.py:68
  78.4 122.6 %all-gather.9.cloned.1.call-done = bf16[5120,1536]{1,0:T(8,128)(2,1)} async-done(((bf16[320,1536]{1,0:T(8,128)(2,1)}), bf16[5120,1536]{1,0:T(8,128)(2,1)}) %all-gather.9.cloned.1.call-update) | async-done | bytes 15728656 | tf_op jit(solution)/shard_map/all_gather | solution.py:78
  201.0 10.8 %fusion.18 = bf16[1,384,1536]{2,1,0:T(8,128)(2,1)S(1)} fusion(bf16[384,5120]{1,0:T(8,128)(2,1)} %all-gather.7.cloned.1.call-done, bf16[5120,1536]{1,0:T(8,128)(2,1)} %all-gather.9.cloned.1.call-done), kind=kOutput, calls=%fused_computation.41 | convolution fusion | flops 6040387584 | bytes 20840448 | tf_op jit(solution)/shard_map/dot_general | solution.py:73
  211.8 110.0 %all-gather.11.cloned.1.call-done = bf16[5120,1536]{1,0:T(8,128)(2,1)} async-done(((bf16[320,1536]{1,0:T(8,128)(2,1)}), bf16[5120,1536]{1,0:T(8,128)(2,1)}) %all-gather.11.cloned.1.call-update) | async-done | bytes 15728656 | tf_op jit(solution)/shard_map/all_gather | solution.py:79
  321.8 10.8 %fusion.19 = bf16[1,384,1536]{2,1,0:T(8,128)(2,1)S(1)} fusion(bf16[384,5120]{1,0:T(8,128)(2,1)} %all-gather.7.cloned.1.call-done, bf16[5120,1536]{1,0:T(8,128)(2,1)} %all-gather.11.cloned.1.call-done), kind=kOutput, calls=%fused_computation.42 | convolution fusion | flops 6040387584 | bytes 20840448 | tf_op jit(solution)/shard_map/dot_general | solution.py:73
  332.6 43.2 %all-gather.13.cloned.1.call-done = bf16[384,5120]{1,0:T(8,128)(2,1)} async-done(((bf16[384,2560]{1,0:T(8,128)(2,1)}), bf16[384,5120]{1,0:T(8,128)(2,1)}) %all-gather.13.cloned.1.call-update) | async-done | bytes 3932176 | tf_op jit(solution)/shard_map/all_gather | solution.py:69
  375.8 10.9 %fusion.20 = bf16[1,384,1536]{2,1,0:T(8,128)(2,1)S(1)} fusion(bf16[384,5120]{1,0:T(8,128)(2,1)} %all-gather.13.cloned.1.call-done, bf16[5120,1536]{1,0:T(8,128)(2,1)} %all-gather.9.cloned.1.call-done), kind=kOutput, calls=%fused_computation.43 | convolution fusion | flops 6040387584 | bytes 20840448 | tf_op jit(solution)/shard_map/dot_general | solution.py:74
  389.0 6.2 fusion.21
  407.3 155.1 %all-gather.15.cloned.1.call-done = bf16[5120,1536]{1,0:T(8,128)(2,1)} async-done(((bf16[320,1536]{1,0:T(8,128)(2,1)}), bf16[5120,1536]{1,0:T(8,128)(2,1)}) %all-gather.15.cloned.1.call-update) | async-done | bytes 15728656 | tf_op jit(solution)/shard_map/all_gather | solution.py:77
  562.3 11.6 %convolution_convert_fusion.2 = bf16[384,1536]{1,0:T(8,128)(2,1)} fusion(bf16[384,5120]{1,0:T(8,128)(2,1)} %all-gather.7.cloned.1.call-done, bf16[5120,1536]{1,0:T(8,128)(2,1)} %all-gather.15.cloned.1.call-done), kind=kOutput, calls=%fused_computation.36 | convolution fusion | flops 6040387584 | bytes 20840448 | tf_op jit(solution)/shard_map/dot_general | solution.py:73
  576.3 11.6 %convolution_convert_fusion.1 = bf16[384,1536]{1,0:T(8,128)(2,1)} fusion(bf16[384,5120]{1,0:T(8,128)(2,1)} %all-gather.13.cloned.1.call-done, bf16[5120,1536]{1,0:T(8,128)(2,1)} %all-gather.15.cloned.1.call-done), kind=kOutput, calls=%fused_computation.35 | convolution fusion | flops 6040387584 | bytes 20840448 | tf_op jit(solution)/shard_map/dot_general | solution.py:74
  590.3 5.9 pad_maximum_fusion
  605.7 5.8 copy.20
  611.5 6.1 copy.31
  617.6 5.8 copy.27
  623.4 13.7 %exponential_reduce_fusion = (f32[12,384]{1,0:T(8,128)}, f32[12,384,1152]{2,1,0:T(8,128)}) fusion(bf16[384,12,128]{0,2,1:T(8,128)(2,1)} %bitcast.66, bf16[1152,12,128]{0,2,1:T(8,128)(2,1)S(1)} %bitcast.55, pred[384,1152]{1,0:T(8,128)(4,1)} %copy.22), kind=kOutput, calls=%fused_computation.7 | convolution fusion | flops 1380189312 | bytes 26413056 | tf_op jit(solution)/shard_map/sub | solution.py:31
  637.0 12.8 %fusion.27 = bf16[12,128,384]{2,1,0:T(8,128)(2,1)} fusion(bf16[1152,12,128]{0,2,1:T(8,128)(2,1)} %bitcast.62, f32[12,384]{1,0:T(8,128)} %get-tuple-element.17, bf16[384,12,128]{0,2,1:T(8,128)(2,1)} %bitcast.67, bf16[1152,12,128]{0,2,1:T(8,128)(2,1)S(1)} %bitcast.56, pred[384,1152]{1,0:T(8,128)(4,1)} %copy.22), kind=kOutput, calls=%fused_computation.49 | convolution fusion | flops 2745046528 | bytes 9897984 | tf_op jit(solution)/shard_map/hqk,khd->qhd/dot_general | solution.py:40
  649.9 12.0 %fusion.36 = f32[12,384,1152]{2,1,0:T(8,128)} fusion(bf16[384,12,128]{0,2,1:T(8,128)(2,1)} %bitcast.60, bf16[1152,12,128]{0,2,1:T(8,128)(2,1)S(1)} %bitcast.57), kind=kOutput, calls=%fused_computation.61 | convolution fusion | flops 1358954496 | bytes 25952256 | tf_op jit(solution)/shard_map/qhd,khd->hqk/dot_general | solution.py:33
  661.8 25.8 %multiply_reduce_fusion = (f32[12,384]{1,0:T(8,128)}, f32[12,384,1152]{2,1,0:T(8,128)}) fusion(f32[12,384]{1,0:T(8,128)S(1)} %copy-done.7, f32[12,384,1152]{2,1,0:T(8,128)} %get-tuple-element.18, f32[12,384,1152]{2,1,0:T(8,128)} %fusion.36, bf16[384,12,128]{0,2,1:T(8,128)(2,1)S(1)} %bitcast.70, bf16[1152,12,128]{0,2,1:T(8,128)(2,1)} %bitcast.64), kind=kOutput, calls=%fused_computation.3 | convolution fusion | flops 1385491968 | bytes 68456448 | tf_op jit(solution)/shard_map/qhd,khd->hqk/dot_general | solution.py:35
  687.6 17.3 %fusion.2 = f32[12,128,384]{2,1,0:T(8,128)} fusion(bf16[1152,12,128]{0,2,1:T(8,128)(2,1)} %bitcast.63, f32[12,384,1152]{2,1,0:T(8,128)} %get-tuple-element.20, f32[12,384]{1,0:T(8,128)} %get-tuple-element.19, f32[12,384]{1,0:T(8,128)} %get-tuple-element.17, bf16[384,12,128]{0,2,1:T(8,128)(2,1)} %bitcast.68, bf16[1152,12,128]{0,2,1:T(8,128)(2,1)S(1)} %bitcast.58, ...), kind=kOutput, calls=%fused_computation.9 | convolution fusion | flops 2755073536 | bytes 32329728 | tf_op jit(solution)/shard_map/hqk,khd->qhd/dot_general | solution.py:46
  704.9 13.4 %add_convert_fusion = bf16[12,128,384]{2,1,0:T(8,128)(2,1)} fusion(f32[12,128,384]{2,1,0:T(8,128)} %fusion.2, bf16[1152,12,128]{0,2,1:T(8,128)(2,1)} %bitcast.61, f32[12,384]{1,0:T(8,128)} %get-tuple-element.17, bf16[384,12,128]{0,2,1:T(8,128)(2,1)} %bitcast.69, bf16[1152,12,128]{0,2,1:T(8,128)(2,1)S(1)} %bitcast.59, pred[384,1152]{1,0:T(8,128)(4,1)} %copy.22), kind=kOutput, calls=%fused_computation.48 | convolution fusion | flops 2745636352 | bytes 12257280 | tf_op jit(solution)/shard_map/hqk,khd->qhd/dot_general | solution.py:43
  718.3 18.4 %convolution_convert_fusion = bf16[768,5120]{1,0:T(8,128)(2,1)} fusion(bf16[1536,5120]{0,1:T(8,128)(2,1)} %all-gather.17.cloned.1.call-done, bf16[384,1536]{0,1:T(8,128)(2,1)} %bitcast.74, bf16[384,1536]{0,1:T(8,128)(2,1)} %bitcast.73), kind=kOutput, calls=%fused_computation.11 | convolution fusion | flops 12088246272 | bytes 25952256 | tf_op jit(solution)/shard_map/dot_general | solution.py:108
  736.8 93.2 %reduce-scatter.2.cloned.1.call-done = bf16[768,2560]{1,0:T(8,128)(2,1)} async-done(((bf16[768,5120]{1,0:T(8,128)(2,1)}), bf16[768,2560]{1,0:T(8,128)(2,1)}) %reduce-scatter.2.cloned.1.call-update) | async-done | bytes 3932176 | tf_op jit(solution)/shard_map/reduce_scatter | solution.py:113
  (55 shorter events, 55.4 us)
Async XLA Ops:
  7.2 9.9 %copy-start = (bf16[384,2560]{1,0:T(8,128)(2,1)S(1)}, bf16[384,2560]{1,0:T(8,128)(2,1)}, u32[]{:S(2)}) copy-start(bf16[384,2560]{1,0:T(8,128)(2,1)} %param.8) | copy-start | bytes 5898244
  7.2 71.2 %all-gather.7.cloned.1.call-start = ((), (), s32[]{:S(2)}) async-start(), calls=%async_computation.1 | async-start | bytes 5898240 | tf_op jit(solution)/shard_map/all_gather | solution.py:68
  22.6 178.4 %all-gather.9.cloned.1.call-start = ((), (), s32[]{:S(2)}) async-start(), calls=%async_computation.2 | async-start | bytes 16711680 | tf_op jit(solution)/shard_map/all_gather | solution.py:78
  23.4 298.4 %all-gather.11.cloned.1.call-start = ((), (), s32[]{:S(2)}) async-start(), calls=%async_computation.3 | async-start | bytes 16711680 | tf_op jit(solution)/shard_map/all_gather | solution.py:79
  24.1 351.7 %all-gather.13.cloned.1.call-start = ((), (), s32[]{:S(2)}) async-start(), calls=%async_computation.4 | async-start | bytes 5898240 | tf_op jit(solution)/shard_map/all_gather | solution.py:69
  24.7 537.6 %all-gather.15.cloned.1.call-start = ((), (), s32[]{:S(2)}) async-start(), calls=%async_computation.5 | async-start | bytes 16711680 | tf_op jit(solution)/shard_map/all_gather | solution.py:77
  25.3 693.0 %all-gather.17.cloned.1.call-start = ((), (), s32[]{:S(2)}) async-start(), calls=%async_computation.6 | async-start | bytes 16711680 | tf_op jit(solution)/shard_map/all_gather | solution.py:110
  25.9 804.2 %reduce-scatter.2.cloned.1.call-start = ((), (), s32[]{:S(2)}) async-start(), calls=%async_computation.7 | async-start | bytes 11796480 | tf_op jit(solution)/shard_map/reduce_scatter | solution.py:113
  375.8 11.8 %copy-start.5 = (bf16[5120,1536]{1,0:T(8,128)(2,1)S(1)}, bf16[5120,1536]{1,0:T(8,128)(2,1)}, u32[]{:S(2)}) copy-start(bf16[5120,1536]{1,0:T(8,128)(2,1)} %all-gather.11.cloned.1.call-done) | copy-start | bytes 47185924
  375.8 13.2 %copy-start.6 = (bf16[384,5120]{1,0:T(8,128)(2,1)S(1)}, bf16[384,5120]{1,0:T(8,128)(2,1)}, u32[]{:S(2)}) copy-start(bf16[384,5120]{1,0:T(8,128)(2,1)} %all-gather.13.cloned.1.call-done) | copy-start | bytes 11796484
  395.2 2.6 copy-start.3
  397.8 192.6 %collective-permute-start = (bf16[4,384,1536]{2,1,0:T(8,128)(2,1)}, bf16[4,384,1536]{2,1,0:T(8,128)(2,1)}, u32[]{:S(2)}, u32[]{:S(2)}) collective-permute-start(bf16[4,384,1536]{2,1,0:T(8,128)(2,1)} %pad_maximum_fusion.1), channel_id=1, source_target_pairs={{0,2},{2,4},{4,6},{6,8},{8,10},{10,12},{12,14},{14,16},{16,18},{18... | collective-permute-start | bytes 14155784 | tf_op jit(solution)/shard_map/ppermute | solution.py:16
  401.5 188.8 %collective-permute-start.1 = (bf16[4,384,1536]{2,1,0:T(8,128)(2,1)}, bf16[4,384,1536]{2,1,0:T(8,128)(2,1)}, u32[]{:S(2)}, u32[]{:S(2)}) collective-permute-start(bf16[4,384,1536]{2,1,0:T(8,128)(2,1)} %pad_maximum_fusion.1), channel_id=1, source_target_pairs={{2,0},{4,2},{6,4},{8,6},{10,8},{12,10},{14,12},{16,14},{18,16},{20... | collective-permute-start | bytes 14155784 | tf_op jit(solution)/shard_map/ppermute | solution.py:19
  649.8 12.0 %copy-start.4 = (bf16[384,1536]{0,1:T(8,128)(2,1)S(1)}, bf16[384,1536]{0,1:T(8,128)(2,1)}, u32[]{:S(2)}) copy-start(bf16[384,1536]{0,1:T(8,128)(2,1)} %copy.23) | copy-start | bytes 3538948
  649.9 12.0 %copy-start.7 = (f32[12,384]{1,0:T(8,128)S(1)}, f32[12,384]{1,0:T(8,128)}, u32[]{:S(2)}) copy-start(f32[12,384]{1,0:T(8,128)} %get-tuple-element.17) | copy-start | bytes 55300
  736.8 96.6 %copy-start.1 = (bf16[384,2560]{1,0:T(8,128)(2,1)S(1)}, bf16[384,2560]{1,0:T(8,128)(2,1)}, u32[]{:S(2)}) copy-start(bf16[384,2560]{1,0:T(8,128)(2,1)} %param.8) | copy-start | bytes 5898244
  830.0 3.3 copy-start.2
Sparse Core Ops, SparseCore 0:
  22.8 55.5 all-gather.6
  80.7 120.2 all-gather.8
  203.3 118.4 all-gather.10
  323.8 51.9 all-gather.12
  377.9 184.3 all-gather.14
  564.5 119.2 all-gather.16
  736.9 93.0 reduce-scatter.1
where the time goes:
time: 855 us; the launch traced here: 851 us
  waiting for transfers between devices  579 us (68%)
  matrix products  175 us (20%)
  local copies, waits for them, and re-layouts  41.5 us (5%)
  other arithmetic  23.4 us (3%)
  between operations  14.5 us (2%)
  blocking collectives  11.3 us (1%)
    all_gather x1, waiting for transfers between devices, shards(): pair_query = add_rows(lax.all_gather(w_query, 'ctx', axis=0, tiled=True))  155 us
    all_gather x1, waiting for transfers between devices, shards(): pair_key = add_rows(lax.all_gather(w_key, 'ctx', axis=0, tiled=True))  123 us
    all_gather x1, waiting for transfers between devices, shards(): pair_value = add_rows(lax.all_gather(w_value, 'ctx', axis=0, tiled=True))  110 us
    reduce_scatter x1, waiting for transfers between devices, shards(): lax.psum_scatter(terms.astype(jnp.bfloat16), 'head', scatter_dimension=1,...  93.2 us
    all_gather x1, waiting for transfers between devices, shards(): lax.all_gather(normed_own, 'head', axis=1, tiled=True)  52.3 us
    all_gather x1, waiting for transfers between devices, shards(): lax.all_gather(normed_t_own, 'head', axis=1, tiled=True)  43.2 us
    dot_general x3, matrix products, add_rows(): first = jnp.dot(normed, weight_rows, preferred_element_type=jnp.float32)  33.2 us
    dot_general x3, matrix products, add_rows(): second = jnp.dot(normed_t, weight_rows, preferred_element_type=jnp.float32)  28.8 us
  transfers between devices with their start and end apart: 9, of which 6 were waited for; matrix products, arithmetic and copies ran while one was open for 24% of the time, Pallas kernels for 0%

commit v1 on v0

--- a/solution.py
+++ b/solution.py
@@ -76,7 +76,29 @@
 
     pair_query = add_rows(lax.all_gather(w_query, "ctx", axis=0, tiled=True))
     pair_key = add_rows(lax.all_gather(w_key, "ctx", axis=0, tiled=True))
-    pair_value = add_rows(lax.all_gather(w_value, "ctx", axis=0, tiled=True))
+
+    def _do_bands(packet, bus_axis, axis_no):
+        slots = lax.psum(1, bus_axis)
+        pages = [(no, (no + 1) % slots) for no in range(slots)]
+        stack_in = [(no, (no - 1) % slots) for no in range(slots)]
+        e_now, oldest = ([packet], [packet])
+        for _ in range(slots // 2):
+            mat_out = lax.ppermute(e_now[-1], bus_axis, pages)
+            e_now.append(mat_out)
+        i0 = 0
+        while i0 < (slots - 1) // 2:
+            moved = lax.ppermute(oldest[-1], bus_axis, stack_in)
+            oldest.append(moved)
+            i0 += 1
+        row_out = jnp.concatenate([*e_now[::-1], *oldest[1:]], axis=axis_no)
+        big = jnp.roll(
+            row_out,
+            shift=(lax.axis_index(bus_axis) - slots // 2) * packet.shape[axis_no],
+            axis=axis_no,
+        )
+        return big
+
+    pair_value = add_rows(_do_bands(w_value, "ctx", 0))
     heads_dev = head_cols // HD
     query = pair_query[0].astype(jnp.bfloat16).reshape(tok_rows, heads_dev, HD)
     query_t = pair_query[1].astype(jnp.bfloat16).reshape(tok_rows, heads_dev, HD)

time: 855 us -> 763 us (0.89)
  waiting for transfers between devices: 579 us -> 317 us
  starting transfers between devices: 5.66 us -> 121 us
  local copies, waits for them, and re-layouts: 41.5 us -> 92.7 us
    all_gather x1, waiting for transfers between devices: 123 us -> 5.97 us  [shards(): pair_key = add_rows(lax.all_gather(w_key, 'ctx', axis=0, tiled=True))]
    ppermute x0 -> x15, starting transfers between devices: none -> 112 us  [the longest x8 103 us: _do_bands(): mat_out = lax.ppermute(e_now[-1], bus_axis, pages)]
    all_gather x1 -> x0, waiting for transfers between devices: 110 us -> none  [shards(): pair_value = add_rows(lax.all_gather(w_value, 'ctx', axis=0, tiled=True))]
    ppermute x0 -> x15, waiting for transfers between devices: none -> 65.9 us  [the longest x8 49.8 us: _do_bands(): mat_out = lax.ppermute(e_now[-1], bus_axis, pages)]
    all_gather x1, waiting for transfers between devices: 52.3 us -> 0.01 us  [shards(): lax.all_gather(normed_own, 'head', axis=1, tiled=True)]
    unnamed x19 -> x82, local copies, waits for them, and re-layouts: 2.36 us -> 52.6 us
    all_gather x1, waiting for transfers between devices: 43.2 us -> 0.02 us  [shards(): lax.all_gather(normed_t_own, 'head', axis=1, tiled=True)]
  transfers between devices with their start and end apart: 9 -> 23, of which waited for: 6 -> 13; matrix products, arithmetic and copies ran while one was open for 24% -> 33% of each run, Pallas kernels for 0% -> 0%
where the time goes in v1:
time: 763 us; the launch traced here: 758 us
  waiting for transfers between devices  317 us (42%)
  matrix products  177 us (23%)
  starting transfers between devices  121 us (16%)
  local copies, waits for them, and re-layouts  92.7 us (12%)
  other arithmetic  23.8 us (3%)
  between operations  14.8 us (2%)
  blocking collectives  11.3 us (1%)
    all_gather x1, waiting for transfers between devices, shards(): pair_query = add_rows(lax.all_gather(w_query, 'ctx', axis=0, tiled=True))  150 us
    ppermute x8, starting transfers between devices, _do_bands(): mat_out = lax.ppermute(e_now[-1], bus_axis, pages)  103 us
    reduce_scatter x1, waiting for transfers between devices, shards(): lax.psum_scatter(terms.astype(jnp.bfloat16), 'head', scatter_dimension=1,...  93.4 us
    unnamed x82, local copies, waits for them, and re-layouts  52.6 us
    ppermute x8, waiting for transfers between devices, _do_bands(): mat_out = lax.ppermute(e_now[-1], bus_axis, pages)  49.8 us
    dot_general x3, matrix products, add_rows(): first = jnp.dot(normed, weight_rows, preferred_element_type=jnp.float32)  34.5 us
    dot_general x3, matrix products, add_rows(): second = jnp.dot(normed_t, weight_rows, preferred_element_type=jnp.float32)  28.8 us
    dot_general x1, matrix products, attend_block(): jnp.einsum('qhd,khd->hqk', queries, keys_t, preferred_element_type=jnp.fl...  25.8 us
  transfers between devices with their start and end apart: 23, of which 13 were waited for; matrix products, arithmetic and copies ran while one was open for 33% of the time, Pallas kernels for 0%

profile of v1, /device:TPU:0, one launch (start us, length us, event | category | flops | bytes accessed | tf_op | source)
XLA Modules:
  0.0 757.8 jit_solution(14548263682084588059)
XLA Ops:
  25.3 16.2 %collective-permute-done = bf16[320,1536]{1,0:T(8,128)(2,1)S(1)} collective-permute-done((bf16[320,1536]{1,0:T(8,128)(2,1)S(1)}, bf16[320,1536]{1,0:T(8,128)(2,1)S(1)}, u32[]{:S(2)}, u32[]{:S(2)}) %collective-permute-start) | collective-permute-done | bytes 983072 | tf_op jit(solution)/shard_map/ppermute | solution.py:86
  46.0 11.9 %collective-permute-done.1 = bf16[320,1536]{1,0:T(8,128)(2,1)S(1)} collective-permute-done((bf16[320,1536]{1,0:T(8,128)(2,1)S(1)}, bf16[320,1536]{1,0:T(8,128)(2,1)S(1)}, u32[]{:S(2)}, u32[]{:S(2)}) %collective-permute-start.1) | collective-permute-done | bytes 983072 | tf_op jit(solution)/shard_map/ppermute | solution.py:86
  62.6 11.6 %collective-permute-done.2 = bf16[320,1536]{1,0:T(8,128)(2,1)S(1)} collective-permute-done((bf16[320,1536]{1,0:T(8,128)(2,1)S(1)}, bf16[320,1536]{1,0:T(8,128)(2,1)S(1)}, u32[]{:S(2)}, u32[]{:S(2)}) %collective-permute-start.2) | collective-permute-done | bytes 983072 | tf_op jit(solution)/shard_map/ppermute | solution.py:86
  74.2 11.7 %collective-permute-start.3 = (bf16[320,1536]{1,0:T(8,128)(2,1)S(1)}, bf16[320,1536]{1,0:T(8,128)(2,1)S(1)}, u32[]{:S(2)}, u32[]{:S(2)}) collective-permute-start(bf16[320,1536]{1,0:T(8,128)(2,1)S(1)} %collective-permute-done.2), channel_id=1, source_target_pairs={{0,2},{2,4},{4,6},{6,8},{8,10},{10,12},{12,14},{14,16},{16,18},{18... | collective-permute-start | bytes 2949128 | tf_op jit(solution)/shard_map/ppermute | solution.py:86
  90.5 18.7 %collective-permute-start.4 = (bf16[320,1536]{1,0:T(8,128)(2,1)S(1)}, bf16[320,1536]{1,0:T(8,128)(2,1)S(1)}, u32[]{:S(2)}, u32[]{:S(2)}) collective-permute-start(bf16[320,1536]{1,0:T(8,128)(2,1)S(1)} %collective-permute-done.3), channel_id=1, source_target_pairs={{0,2},{2,4},{4,6},{6,8},{8,10},{10,12},{12,14},{14,16},{16,18},{18... | collective-permute-start | bytes 2949128 | tf_op jit(solution)/shard_map/ppermute | solution.py:86
  112.3 20.3 %collective-permute-start.5 = (bf16[320,1536]{1,0:T(8,128)(2,1)S(1)}, bf16[320,1536]{1,0:T(8,128)(2,1)S(1)}, u32[]{:S(2)}, u32[]{:S(2)}) collective-permute-start(bf16[320,1536]{1,0:T(8,128)(2,1)S(1)} %collective-permute-done.4), channel_id=1, source_target_pairs={{0,2},{2,4},{4,6},{6,8},{8,10},{10,12},{12,14},{14,16},{16,18},{18... | collective-permute-start | bytes 2949128 | tf_op jit(solution)/shard_map/ppermute | solution.py:86
  134.7 31.3 %collective-permute-start.6 = (bf16[320,1536]{1,0:T(8,128)(2,1)S(1)}, bf16[320,1536]{1,0:T(8,128)(2,1)}, u32[]{:S(2)}, u32[]{:S(2)}) collective-permute-start(bf16[320,1536]{1,0:T(8,128)(2,1)S(1)} %collective-permute-done.5), channel_id=1, source_target_pairs={{0,2},{2,4},{4,6},{6,8},{8,10},{10,12},{12,14},{14,16},{16,18},{18... | collective-permute-start | bytes 2949128 | tf_op jit(solution)/shard_map/ppermute | solution.py:86
  168.3 15.9 %collective-permute-start.7 = (bf16[320,1536]{1,0:T(8,128)(2,1)}, bf16[320,1536]{1,0:T(8,128)(2,1)}, u32[]{:S(2)}, u32[]{:S(2)}) collective-permute-start(bf16[320,1536]{1,0:T(8,128)(2,1)} %collective-permute-done.6), channel_id=1, source_target_pairs={{0,2},{2,4},{4,6},{6,8},{8,10},{10,12},{12,14},{14,16},{16,18},{18... | collective-permute-start | bytes 2949128 | tf_op jit(solution)/shard_map/ppermute | solution.py:86
  184.4 9.4 %collective-permute-done.13 = bf16[320,1536]{1,0:T(8,128)(2,1)} collective-permute-done((bf16[320,1536]{1,0:T(8,128)(2,1)}, bf16[320,1536]{1,0:T(8,128)(2,1)}, u32[]{:S(2)}, u32[]{:S(2)}) %collective-permute-start.13) | collective-permute-done | bytes 983072 | tf_op jit(solution)/shard_map/ppermute | solution.py:90
  253.9 11.6 %fusion.33 = bf16[1,384,1536]{2,1,0:T(8,128)(2,1)S(1)} fusion(bf16[384,5120]{1,0:T(8,128)(2,1)} %all-gather.6.cloned.1.call-done, bf16[10240,1536]{1,0:T(8,128)(2,1)} %constant_dynamic-update-slice_fusion, s32[]{:T(128)S(6)} %select_n.29), kind=kOutput, calls=%fused_computation.48 | convolution fusion | flops 6040387584 | bytes 20840452 | tf_op jit(solution)/shard_map/dot_general | solution.py:73
  265.5 11.0 %fusion.30 = bf16[1,384,1536]{2,1,0:T(8,128)(2,1)S(1)} fusion(bf16[384,5120]{1,0:T(8,128)(2,1)} %all-gather.10.cloned.1.call-done, bf16[10240,1536]{1,0:T(8,128)(2,1)} %constant_dynamic-update-slice_fusion, s32[]{:T(128)S(6)} %select_n.29), kind=kOutput, calls=%fused_computation.47 | convolution fusion | flops 6040387584 | bytes 20840452 | tf_op jit(solution)/shard_map/dot_general | solution.py:74
  282.5 11.3 %fusion.28 = bf16[1,384,1536]{2,1,0:T(8,128)(2,1)S(1)} fusion(bf16[384,5120]{1,0:T(8,128)(2,1)} %all-gather.6.cloned.1.call-done, bf16[5120,1536]{1,0:T(8,128)(2,1)} %all-gather.8.cloned.1.call-done), kind=kOutput, calls=%fused_computation.45 | convolution fusion | flops 6040387584 | bytes 20840448 | tf_op jit(solution)/shard_map/dot_general | solution.py:73
  305.3 8.0 %collective-permute-start.15 = (bf16[4,384,1536]{2,1,0:T(8,128)(2,1)}, bf16[4,384,1536]{2,1,0:T(8,128)(2,1)}, u32[]{:S(2)}, u32[]{:S(2)}) collective-permute-start(bf16[4,384,1536]{2,1,0:T(8,128)(2,1)} %pad_maximum_fusion.1), channel_id=1, source_target_pairs={{0,2},{2,4},{4,6},{6,8},{8,10},{10,12},{12,14},{14,16},{16,18},{18... | collective-permute-start | bytes 14155784 | tf_op jit(solution)/shard_map/ppermute | solution.py:16
  318.9 149.7 %all-gather.12.cloned.1.call-done = bf16[5120,1536]{1,0:T(8,128)(2,1)} async-done(((bf16[320,1536]{1,0:T(8,128)(2,1)}), bf16[5120,1536]{1,0:T(8,128)(2,1)}) %all-gather.12.cloned.1.call-update) | async-done | bytes 15728656 | tf_op jit(solution)/shard_map/all_gather | solution.py:77
  468.6 11.6 %convolution_convert_fusion.2 = bf16[384,1536]{1,0:T(8,128)(2,1)} fusion(bf16[384,5120]{1,0:T(8,128)(2,1)} %all-gather.6.cloned.1.call-done, bf16[5120,1536]{1,0:T(8,128)(2,1)} %all-gather.12.cloned.1.call-done), kind=kOutput, calls=%fused_computation.42 | convolution fusion | flops 6040387584 | bytes 20840448 | tf_op jit(solution)/shard_map/dot_general | solution.py:73
  482.5 11.6 %convolution_convert_fusion.1 = bf16[384,1536]{1,0:T(8,128)(2,1)} fusion(bf16[384,5120]{1,0:T(8,128)(2,1)} %all-gather.10.cloned.1.call-done, bf16[5120,1536]{1,0:T(8,128)(2,1)} %all-gather.12.cloned.1.call-done), kind=kOutput, calls=%fused_computation.41 | convolution fusion | flops 6040387584 | bytes 20840448 | tf_op jit(solution)/shard_map/dot_general | solution.py:74
  529.6 13.6 %exponential_reduce_fusion = (f32[12,384]{1,0:T(8,128)}, f32[12,384,1152]{2,1,0:T(8,128)}) fusion(bf16[384,12,128]{0,2,1:T(8,128)(2,1)} %bitcast.64, bf16[1152,12,128]{0,2,1:T(8,128)(2,1)S(1)} %bitcast.53, pred[384,1152]{1,0:T(8,128)(4,1)} %copy.22), kind=kOutput, calls=%fused_computation.7 | convolution fusion | flops 1380189312 | bytes 26413056 | tf_op jit(solution)/shard_map/sub | solution.py:31
  543.2 12.8 %fusion.41 = bf16[12,128,384]{2,1,0:T(8,128)(2,1)} fusion(bf16[1152,12,128]{0,2,1:T(8,128)(2,1)} %bitcast.60, f32[12,384]{1,0:T(8,128)} %get-tuple-element.17, bf16[384,12,128]{0,2,1:T(8,128)(2,1)} %bitcast.65, bf16[1152,12,128]{0,2,1:T(8,128)(2,1)S(1)} %bitcast.54, pred[384,1152]{1,0:T(8,128)(4,1)} %copy.22), kind=kOutput, calls=%fused_computation.53 | convolution fusion | flops 2745046528 | bytes 9897984 | tf_op jit(solution)/shard_map/hqk,khd->qhd/dot_general | solution.py:40
  556.0 12.0 %fusion.52 = f32[12,384,1152]{2,1,0:T(8,128)} fusion(bf16[384,12,128]{0,2,1:T(8,128)(2,1)} %bitcast.58, bf16[1152,12,128]{0,2,1:T(8,128)(2,1)S(1)} %bitcast.55), kind=kOutput, calls=%fused_computation.99 | convolution fusion | flops 1358954496 | bytes 25952256 | tf_op jit(solution)/shard_map/qhd,khd->hqk/dot_general | solution.py:33
  568.0 25.8 %multiply_reduce_fusion = (f32[12,384]{1,0:T(8,128)}, f32[12,384,1152]{2,1,0:T(8,128)}) fusion(f32[12,384]{1,0:T(8,128)S(1)} %copy-done.23, f32[12,384,1152]{2,1,0:T(8,128)} %get-tuple-element.18, f32[12,384,1152]{2,1,0:T(8,128)} %fusion.52, bf16[384,12,128]{0,2,1:T(8,128)(2,1)S(1)} %bitcast.68, bf16[1152,12,128]{0,2,1:T(8,128)(2,1)} %bitcast.62), kind=kOutput, calls=%fused_computation.3 | convolution fusion | flops 1385491968 | bytes 68456448 | tf_op jit(solution)/shard_map/qhd,khd->hqk/dot_general | solution.py:35
  593.8 17.4 %fusion.6 = f32[12,128,384]{2,1,0:T(8,128)} fusion(bf16[1152,12,128]{0,2,1:T(8,128)(2,1)} %bitcast.61, f32[12,384,1152]{2,1,0:T(8,128)} %get-tuple-element.20, f32[12,384]{1,0:T(8,128)} %get-tuple-element.19, f32[12,384]{1,0:T(8,128)} %get-tuple-element.17, bf16[384,12,128]{0,2,1:T(8,128)(2,1)} %bitcast.66, bf16[1152,12,128]{0,2,1:T(8,128)(2,1)S(1)} %bitcast.56, ...), kind=kOutput, calls=%fused_computation.13 | convolution fusion | flops 2755073536 | bytes 32329728 | tf_op jit(solution)/shard_map/hqk,khd->qhd/dot_general | solution.py:46
  611.3 13.4 %add_convert_fusion = bf16[12,128,384]{2,1,0:T(8,128)(2,1)} fusion(f32[12,128,384]{2,1,0:T(8,128)} %fusion.6, bf16[1152,12,128]{0,2,1:T(8,128)(2,1)} %bitcast.59, f32[12,384]{1,0:T(8,128)} %get-tuple-element.17, bf16[384,12,128]{0,2,1:T(8,128)(2,1)} %bitcast.67, bf16[1152,12,128]{0,2,1:T(8,128)(2,1)S(1)} %bitcast.57, pred[384,1152]{1,0:T(8,128)(4,1)} %copy.22), kind=kOutput, calls=%fused_computation.52 | convolution fusion | flops 2745636352 | bytes 12257280 | tf_op jit(solution)/shard_map/hqk,khd->qhd/dot_general | solution.py:43
  624.7 18.4 %convolution_convert_fusion = bf16[768,5120]{1,0:T(8,128)(2,1)} fusion(bf16[1536,5120]{0,1:T(8,128)(2,1)} %all-gather.14.cloned.1.call-done, bf16[384,1536]{0,1:T(8,128)(2,1)} %bitcast.72, bf16[384,1536]{0,1:T(8,128)(2,1)} %bitcast.71), kind=kOutput, calls=%fused_computation.15 | convolution fusion | flops 12088246272 | bytes 25952256 | tf_op jit(solution)/shard_map/dot_general | solution.py:130
  643.2 93.4 %reduce-scatter.2.cloned.1.call-done = bf16[768,2560]{1,0:T(8,128)(2,1)} async-done(((bf16[768,5120]{1,0:T(8,128)(2,1)}), bf16[768,2560]{1,0:T(8,128)(2,1)}) %reduce-scatter.2.cloned.1.call-update) | async-done | bytes 3932176 | tf_op jit(solution)/shard_map/reduce_scatter | solution.py:135
  (146 shorter events, 174.4 us)
Async XLA Ops:
  7.2 246.8 %all-gather.6.cloned.1.call-start = ((), (), s32[]{:S(2)}) async-start(), calls=%async_computation.1 | async-start | bytes 5898240 | tf_op jit(solution)/shard_map/all_gather | solution.py:68
  23.2 242.4 %all-gather.10.cloned.1.call-start = ((), (), s32[]{:S(2)}) async-start(), calls=%async_computation.3 | async-start | bytes 5898240 | tf_op jit(solution)/shard_map/all_gather | solution.py:69
  23.9 258.6 %all-gather.8.cloned.1.call-start = ((), (), s32[]{:S(2)}) async-start(), calls=%async_computation.2 | async-start | bytes 16711680 | tf_op jit(solution)/shard_map/all_gather | solution.py:78
  24.6 443.9 %all-gather.12.cloned.1.call-start = ((), (), s32[]{:S(2)}) async-start(), calls=%async_computation.4 | async-start | bytes 16711680 | tf_op jit(solution)/shard_map/all_gather | solution.py:77
  25.2 599.5 %all-gather.14.cloned.1.call-start = ((), (), s32[]{:S(2)}) async-start(), calls=%async_computation.5 | async-start | bytes 16711680 | tf_op jit(solution)/shard_map/all_gather | solution.py:132
  25.3 16.3 %collective-permute-start = (bf16[320,1536]{1,0:T(8,128)(2,1)S(1)}, bf16[320,1536]{1,0:T(8,128)(2,1)S(1)}, u32[]{:S(2)}, u32[]{:S(2)}) collective-permute-start(bf16[320,1536]{1,0:T(8,128)(2,1)S(1)} %copy-done.3), channel_id=1, source_target_pairs={{0,2},{2,4},{4,6},{6,8},{8,10},{10,12},{12,14},{14,16},{16,18},{18... | collective-permute-start | bytes 2949128 | tf_op jit(solution)/shard_map/ppermute | solution.py:86
  41.6 16.3 %collective-permute-start.1 = (bf16[320,1536]{1,0:T(8,128)(2,1)S(1)}, bf16[320,1536]{1,0:T(8,128)(2,1)S(1)}, u32[]{:S(2)}, u32[]{:S(2)}) collective-permute-start(bf16[320,1536]{1,0:T(8,128)(2,1)S(1)} %collective-permute-done), channel_id=1, source_target_pairs={{0,2},{2,4},{4,6},{6,8},{8,10},{10,12},{12,14},{14,16},{16,18},{18... | collective-permute-start | bytes 2949128 | tf_op jit(solution)/shard_map/ppermute | solution.py:86
  41.6 21.0 %collective-permute-start.8 = (bf16[320,1536]{1,0:T(8,128)(2,1)S(1)}, bf16[320,1536]{1,0:T(8,128)(2,1)S(1)}, u32[]{:S(2)}, u32[]{:S(2)}) collective-permute-start(bf16[320,1536]{1,0:T(8,128)(2,1)S(1)} %copy-done.3), channel_id=1, source_target_pairs={{0,30},{2,0},{4,2},{6,4},{8,6},{10,8},{12,10},{14,12},{16,14},{18,... | collective-permute-start | bytes 2949128 | tf_op jit(solution)/shard_map/ppermute | solution.py:90
  57.9 16.3 %collective-permute-start.2 = (bf16[320,1536]{1,0:T(8,128)(2,1)S(1)}, bf16[320,1536]{1,0:T(8,128)(2,1)S(1)}, u32[]{:S(2)}, u32[]{:S(2)}) collective-permute-start(bf16[320,1536]{1,0:T(8,128)(2,1)S(1)} %collective-permute-done.1), channel_id=1, source_target_pairs={{0,2},{2,4},{4,6},{6,8},{8,10},{10,12},{12,14},{14,16},{16,18},{18... | collective-permute-start | bytes 2949128 | tf_op jit(solution)/shard_map/ppermute | solution.py:86
  62.6 23.3 %collective-permute-start.9 = (bf16[320,1536]{1,0:T(8,128)(2,1)S(1)}, bf16[320,1536]{1,0:T(8,128)(2,1)S(1)}, u32[]{:S(2)}, u32[]{:S(2)}) collective-permute-start(bf16[320,1536]{1,0:T(8,128)(2,1)S(1)} %collective-permute-done.8), channel_id=1, source_target_pairs={{0,30},{2,0},{4,2},{6,4},{8,6},{10,8},{12,10},{14,12},{16,14},{18,... | collective-permute-start | bytes 2949128 | tf_op jit(solution)/shard_map/ppermute | solution.py:90
  74.2 16.3 %collective-permute-start.3 = (bf16[320,1536]{1,0:T(8,128)(2,1)S(1)}, bf16[320,1536]{1,0:T(8,128)(2,1)S(1)}, u32[]{:S(2)}, u32[]{:S(2)}) collective-permute-start(bf16[320,1536]{1,0:T(8,128)(2,1)S(1)} %collective-permute-done.2), channel_id=1, source_target_pairs={{0,2},{2,4},{4,6},{6,8},{8,10},{10,12},{12,14},{14,16},{16,18},{18... | collective-permute-start | bytes 2949128 | tf_op jit(solution)/shard_map/ppermute | solution.py:86
  85.9 23.3 %collective-permute-start.10 = (bf16[320,1536]{1,0:T(8,128)(2,1)S(1)}, bf16[320,1536]{1,0:T(8,128)(2,1)S(1)}, u32[]{:S(2)}, u32[]{:S(2)}) collective-permute-start(bf16[320,1536]{1,0:T(8,128)(2,1)S(1)} %collective-permute-done.9), channel_id=1, source_target_pairs={{0,30},{2,0},{4,2},{6,4},{8,6},{10,8},{12,10},{14,12},{16,14},{18,... | collective-permute-start | bytes 2949128 | tf_op jit(solution)/shard_map/ppermute | solution.py:90
  90.5 21.7 %collective-permute-start.4 = (bf16[320,1536]{1,0:T(8,128)(2,1)S(1)}, bf16[320,1536]{1,0:T(8,128)(2,1)S(1)}, u32[]{:S(2)}, u32[]{:S(2)}) collective-permute-start(bf16[320,1536]{1,0:T(8,128)(2,1)S(1)} %collective-permute-done.3), channel_id=1, source_target_pairs={{0,2},{2,4},{4,6},{6,8},{8,10},{10,12},{12,14},{14,16},{16,18},{18... | collective-permute-start | bytes 2949128 | tf_op jit(solution)/shard_map/ppermute | solution.py:86
  109.2 23.3 %collective-permute-start.11 = (bf16[320,1536]{1,0:T(8,128)(2,1)S(1)}, bf16[320,1536]{1,0:T(8,128)(2,1)S(1)}, u32[]{:S(2)}, u32[]{:S(2)}) collective-permute-start(bf16[320,1536]{1,0:T(8,128)(2,1)S(1)} %collective-permute-done.10), channel_id=1, source_target_pairs={{0,30},{2,0},{4,2},{6,4},{8,6},{10,8},{12,10},{14,12},{16,14},{18,... | collective-permute-start | bytes 2949128 | tf_op jit(solution)/shard_map/ppermute | solution.py:90
  112.3 22.5 %collective-permute-start.5 = (bf16[320,1536]{1,0:T(8,128)(2,1)S(1)}, bf16[320,1536]{1,0:T(8,128)(2,1)S(1)}, u32[]{:S(2)}, u32[]{:S(2)}) collective-permute-start(bf16[320,1536]{1,0:T(8,128)(2,1)S(1)} %collective-permute-done.4), channel_id=1, source_target_pairs={{0,2},{2,4},{4,6},{6,8},{8,10},{10,12},{12,14},{14,16},{16,18},{18... | collective-permute-start | bytes 2949128 | tf_op jit(solution)/shard_map/ppermute | solution.py:86
  133.5 32.5 %collective-permute-start.12 = (bf16[320,1536]{1,0:T(8,128)(2,1)S(1)}, bf16[320,1536]{1,0:T(8,128)(2,1)}, u32[]{:S(2)}, u32[]{:S(2)}) collective-permute-start(bf16[320,1536]{1,0:T(8,128)(2,1)S(1)} %collective-permute-done.11), channel_id=1, source_target_pairs={{0,30},{2,0},{4,2},{6,4},{8,6},{10,8},{12,10},{14,12},{16,14},{18,... | collective-permute-start | bytes 2949128 | tf_op jit(solution)/shard_map/ppermute | solution.py:90
  134.7 33.6 %collective-permute-start.6 = (bf16[320,1536]{1,0:T(8,128)(2,1)S(1)}, bf16[320,1536]{1,0:T(8,128)(2,1)}, u32[]{:S(2)}, u32[]{:S(2)}) collective-permute-start(bf16[320,1536]{1,0:T(8,128)(2,1)S(1)} %collective-permute-done.5), channel_id=1, source_target_pairs={{0,2},{2,4},{4,6},{6,8},{8,10},{10,12},{12,14},{14,16},{16,18},{18... | collective-permute-start | bytes 2949128 | tf_op jit(solution)/shard_map/ppermute | solution.py:86
  166.0 27.8 %collective-permute-start.13 = (bf16[320,1536]{1,0:T(8,128)(2,1)}, bf16[320,1536]{1,0:T(8,128)(2,1)}, u32[]{:S(2)}, u32[]{:S(2)}) collective-permute-start(bf16[320,1536]{1,0:T(8,128)(2,1)} %collective-permute-done.12), channel_id=1, source_target_pairs={{0,30},{2,0},{4,2},{6,4},{8,6},{10,8},{12,10},{14,12},{16,14},{18,... | collective-permute-start | bytes 2949128 | tf_op jit(solution)/shard_map/ppermute | solution.py:90
  168.3 31.2 %collective-permute-start.7 = (bf16[320,1536]{1,0:T(8,128)(2,1)}, bf16[320,1536]{1,0:T(8,128)(2,1)}, u32[]{:S(2)}, u32[]{:S(2)}) collective-permute-start(bf16[320,1536]{1,0:T(8,128)(2,1)} %collective-permute-done.6), channel_id=1, source_target_pairs={{0,2},{2,4},{4,6},{6,8},{8,10},{10,12},{12,14},{14,16},{16,18},{18... | collective-permute-start | bytes 2949128 | tf_op jit(solution)/shard_map/ppermute | solution.py:86
  184.3 552.3 %reduce-scatter.2.cloned.1.call-start = ((), (), s32[]{:S(2)}) async-start(), calls=%async_computation.6 | async-start | bytes 11796480 | tf_op jit(solution)/shard_map/reduce_scatter | solution.py:135
  193.8 37.8 %collective-permute-start.14 = (bf16[320,1536]{1,0:T(8,128)(2,1)}, bf16[320,1536]{1,0:T(8,128)(2,1)S(1)}, u32[]{:S(2)}, u32[]{:S(2)}) collective-permute-start(bf16[320,1536]{1,0:T(8,128)(2,1)} %collective-permute-done.13), channel_id=1, source_target_pairs={{0,30},{2,0},{4,2},{6,4},{8,6},{10,8},{12,10},{14,12},{16,14},{18,... | collective-permute-start | bytes 2949128 | tf_op jit(solution)/shard_map/ppermute | solution.py:90
  305.3 191.2 %collective-permute-start.15 = (bf16[4,384,1536]{2,1,0:T(8,128)(2,1)}, bf16[4,384,1536]{2,1,0:T(8,128)(2,1)}, u32[]{:S(2)}, u32[]{:S(2)}) collective-permute-start(bf16[4,384,1536]{2,1,0:T(8,128)(2,1)} %pad_maximum_fusion.1), channel_id=1, source_target_pairs={{0,2},{2,4},{4,6},{6,8},{8,10},{10,12},{12,14},{14,16},{16,18},{18... | collective-permute-start | bytes 14155784 | tf_op jit(solution)/shard_map/ppermute | solution.py:16
  313.3 183.2 %collective-permute-start.16 = (bf16[4,384,1536]{2,1,0:T(8,128)(2,1)}, bf16[4,384,1536]{2,1,0:T(8,128)(2,1)}, u32[]{:S(2)}, u32[]{:S(2)}) collective-permute-start(bf16[4,384,1536]{2,1,0:T(8,128)(2,1)} %pad_maximum_fusion.1), channel_id=1, source_target_pairs={{2,0},{4,2},{6,4},{8,6},{10,8},{12,10},{14,12},{16,14},{18,16},{20... | collective-permute-start | bytes 14155784 | tf_op jit(solution)/shard_map/ppermute | solution.py:19
  643.1 96.8 %copy-start = (bf16[384,2560]{1,0:T(8,128)(2,1)S(1)}, bf16[384,2560]{1,0:T(8,128)(2,1)}, u32[]{:S(2)}) copy-start(bf16[384,2560]{1,0:T(8,128)(2,1)} %param.8) | copy-start | bytes 5898244
  (23 other events, 504.6 us)
Sparse Core Ops, SparseCore 0:
  23.3 55.5 all-gather.5
  81.0 53.7 all-gather.9
  137.1 145.2 all-gather.7
  284.6 183.8 all-gather.11
  470.7 119.3 all-gather.13
  643.3 93.2 reduce-scatter.1
